TPU v7x, 32 devices: a whole 2x2x4 slice. The times are simulated.
32 devices in a mesh: db: 16 (over z, x, core), mp: 2 (over y).
Axes of the slice: x: 2, y: 2, z: 4, core: 2. Of those that a mesh axis runs over, the one named last changes fastest.
Arguments:
- queries: bfloat16 [32768, 2048], P('db', 'mp'), may hold values from -400 to 400, as said below
- encodings: bfloat16 [512, 128, 896], P(('db', 'mp')), may hold values from -6 to 6
- key_weight: bfloat16 [896, 2048], P('db', 'mp'), may hold values from -0.1875 to 0.1875
- value_weight: bfloat16 [896, 2048], P('db', 'mp'), may hold values from -0.1875 to 0.1875
- nbr_shard: int32 [512, 2], P('db'), may hold values from 0 to 15, all different within a row; in each aligned block of 32 rows (0 to 31, 32 to 63, ...) at most 8 rows name the same one
- nbr_row: int32 [512, 2], P('db'), may hold values from 0 to 31
Outputs:
- cross_out: bfloat16 [32768, 2048], P('db', 'mp')
Inputs may be any that keep to these rules, and one draw needn't show every extreme that they name: `queries`: some query rows may be far larger than the rest. `nbr_shard`: among the spans of one index of db no shard is named by more than 8 spans; the 2 shards of one span differ.
All inputs are finite; a program needn't handle non-finite values.
Results may differ from a plain program's by a relative error of at most 0.025.
Values may be sent and summed in bfloat16 or wider, within the bound.
No kernel may reach another device: no remote copies, remote signals or barrier semaphores. Data moves between devices by JAX's collectives and lax.ppermute only.
A program may use at most 256 MiB of HBM per device.

v0:
```python
import math
import jax
import jax.numpy as jnp
from jax import lax
from jax.sharding import PartitionSpec as P

DH = 128
SPAN = 64
SEQ = 128


def attend(queried, key_block, value_block, head_dim):
    batch_size, length, columns = queried.shape
    head_count = columns // head_dim
    query_heads = queried.reshape(batch_size, length, head_count, head_dim)
    key_heads = key_block.reshape(batch_size, key_block.shape[1], head_count, head_dim)
    value_heads = value_block.reshape(batch_size, value_block.shape[1], head_count, head_dim)
    scores = jnp.einsum(
        "bqhd,bkhd->bhqk", query_heads, key_heads, preferred_element_type=jnp.float32
    ) * (1.0 / math.sqrt(head_dim))
    row_max = jnp.max(scores, axis=-1)
    expscore = jnp.exp(scores - row_max[..., None])
    row_sum = jnp.sum(expscore, axis=-1)
    partial_value = jnp.einsum(
        "bhqk,bkhd->bqhd",
        expscore.astype(jnp.bfloat16),
        value_heads,
        preferred_element_type=jnp.float32,
    )
    return (
        partial_value.reshape(batch_size, length, columns).astype(jnp.bfloat16),
        row_max,
        row_sum,
    )


def local(queries, encodings, key_weight, value_weight, nbr_shard, nbr_row):
    shards = lax.axis_size("db")
    columns = queries.shape[1]
    head_count = columns // DH
    span_count = nbr_shard.shape[0]
    neighbours = nbr_shard.shape[1]
    capacity = max(2, 4 * span_count // shards)
    slots = shards * capacity
    full_keys, full_values = (
        lax.all_gather(key_weight, "db", axis=0, tiled=True),
        lax.all_gather(value_weight, "db", axis=0, tiled=True),
    )
    both_weights = jnp.concatenate([full_keys, full_values], axis=1)
    piece = lax.all_gather(encodings, "mp", axis=0, tiled=True)
    flat = piece.reshape(piece.shape[0] * piece.shape[1], piece.shape[2])
    mixed = jnp.dot(flat, both_weights, preferred_element_type=jnp.float32).astype(jnp.bfloat16)
    key_value = mixed.reshape(piece.shape[0], piece.shape[1], 2 * columns)
    sequences = queries.shape[0] // SEQ
    seq_rows = queries.reshape(sequences, SEQ, columns)
    shifted = jnp.concatenate(
        [seq_rows[:, SPAN - 1 :], jnp.zeros((sequences, SPAN - 1, columns), jnp.bfloat16)], axis=1
    )
    windows = shifted.reshape(span_count, SPAN * columns)
    want_shard = nbr_shard.reshape(-1)
    want_row = nbr_row.reshape(-1)
    request_count = want_shard.shape[0]
    positions = jnp.arange(request_count, dtype=jnp.int32)
    same_shard = (want_shard[:, None] == want_shard[None, :]) & (
        positions[None, :] < positions[:, None]
    )
    slot_rank = jnp.sum(same_shard.astype(jnp.int32), axis=1)
    slot_index = want_shard * capacity + slot_rank
    onehot_slots = slot_index[:, None] == jnp.arange(slots, dtype=jnp.int32)[None, :]
    send_row = jnp.sum(jnp.where(onehot_slots, want_row[:, None], 0), axis=0).reshape(
        shards, capacity
    )
    selector = jnp.sum(
        onehot_slots.reshape(span_count, neighbours, slots).astype(jnp.bfloat16), axis=1
    )
    send_query = jnp.dot(selector.T, windows, preferred_element_type=jnp.float32).astype(
        jnp.bfloat16
    )
    send_query = send_query.reshape(shards, capacity, SPAN, columns)
    asked = lax.all_to_all(send_query, "db", split_axis=0, concat_axis=0, tiled=True)
    asked_rows = lax.all_to_all(send_row, "db", split_axis=0, concat_axis=0, tiled=True)
    peer_count = asked_rows.shape[0]
    item_count = asked_rows.shape[1]
    group_size = math.gcd(peer_count, 8)
    grouped = asked.reshape(peer_count // group_size, group_size * item_count, SPAN, columns)
    grouped_rows = asked_rows.reshape(peer_count // group_size, group_size * item_count)

    def one_group(operands):
        group_query, group_rows = operands
        picked = jnp.take(key_value, group_rows, axis=0)
        return attend(group_query, picked[..., :columns], picked[..., columns:], DH)

    partial_value, row_max, row_sum = lax.map(one_group, (grouped, grouped_rows))
    partial_value = partial_value.reshape(peer_count, item_count, SPAN, columns)
    row_max = row_max.reshape(peer_count, item_count, head_count, SPAN)
    row_sum = row_sum.reshape(peer_count, item_count, head_count, SPAN)
    partial_value = lax.all_to_all(partial_value, "db", split_axis=0, concat_axis=0, tiled=True)
    row_max, row_sum = (
        lax.all_to_all(row_max, "db", split_axis=0, concat_axis=0, tiled=True),
        lax.all_to_all(row_sum, "db", split_axis=0, concat_axis=0, tiled=True),
    )
    partial_value, row_max, row_sum = (partial_value, row_max, row_sum)
    partial_value = jnp.take(partial_value.reshape(slots, SPAN, columns), slot_index, axis=0)
    row_max = jnp.take(row_max.reshape(slots, head_count, SPAN), slot_index, axis=0)
    row_sum = jnp.take(row_sum.reshape(slots, head_count, SPAN), slot_index, axis=0)
    row_max = row_max.reshape(span_count, neighbours, head_count, SPAN)
    row_sum = row_sum.reshape(span_count, neighbours, head_count, SPAN)
    partial_value = partial_value.reshape(span_count, neighbours, SPAN, head_count, DH).astype(
        jnp.float32
    )
    largest = jnp.max(row_max, axis=1)
    weights_each = jnp.exp(row_max - largest[:, None])
    denominator = jnp.sum(weights_each * row_sum, axis=1)
    numerator = jnp.sum(jnp.swapaxes(weights_each, 2, 3)[..., None] * partial_value, axis=1)
    attended = (numerator / jnp.swapaxes(denominator, 1, 2)[..., None]).astype(jnp.bfloat16)
    attended = attended.reshape(sequences, SEQ, columns)
    result = jnp.concatenate(
        [jnp.zeros((sequences, SPAN - 1, columns), jnp.bfloat16), attended[:, : SEQ - SPAN + 1]],
        axis=1,
    )
    return result.reshape(sequences * SEQ, columns)


def solution(mesh):
    placed = (
        P("db", "mp"),
        P(("db", "mp"), None, None),
        P("db", "mp"),
        P("db", "mp"),
        P("db", None),
        P("db", None),
    )
    return jax.shard_map(
        local, mesh=mesh, in_specs=placed, out_specs=P("db", "mp"), check_vma=False
    )
```

profile of v0, /device:TPU:11, one launch (start us, length us, event | category | flops | bytes accessed | tf_op | source)
XLA Modules:
  0.0 1427.6 jit_solution(8872616640881158538)
XLA Ops:
  9.8 6.5 all-to-all-start
  23.3 5.6 reshape.185
  28.9 12.5 convolution_convert_fusion
  41.4 6.0 all-to-all-start.1
  50.9 175.7 %all-gather.4.cloned.1.call-done = bf16[896,1024]{1,0:T(8,128)(2,1)} async-done(((bf16[56,1024]{1,0:T(8,128)(2,1)}), bf16[896,1024]{1,0:T(8,128)(2,1)}) %all-gather.4.cloned.1.call-update) | async-done | bytes 1835024 | tf_op jit(solution)/shard_map/all_gather | solution.py:46
  226.6 131.3 %all-gather.6.cloned.1.call-done = bf16[896,1024]{1,0:T(8,128)(2,1)} async-done(((bf16[56,1024]{1,0:T(8,128)(2,1)}), bf16[896,1024]{1,0:T(8,128)(2,1)}) %all-gather.6.cloned.1.call-update) | async-done | bytes 1835024 | tf_op jit(solution)/shard_map/all_gather | solution.py:47
  357.9 94.6 %all-gather.8.cloned.1.call-done = bf16[32,128,896]{2,1,0:T(8,128)(2,1)} async-done(((bf16[16,128,896]{2,1,0:T(8,128)(2,1)}), bf16[32,128,896]{2,1,0:T(8,128)(2,1)}) %all-gather.8.cloned.1.call-update) | async-done | bytes 7340048 | tf_op jit(solution)/shard_map/all_gather | solution.py:50
  452.5 24.3 %convert_bitcast_fusion.1 = bf16[4096,2048]{0,1:T(8,128)(2,1)} fusion(bf16[4096,896]{1,0:T(8,128)(2,1)} %bitcast.105, bf16[896,1024]{1,0:T(8,128)(2,1)} %all-gather.6.cloned.1.call-done, bf16[896,1024]{1,0:T(8,128)(2,1)} %all-gather.4.cloned.1.call-done), kind=kOutput, calls=%fused_computation.28 | convolution fusion | flops 15048114176 | bytes 27787264 | tf_op jit(solution)/shard_map/dot_general | solution.py:52
  476.8 22.2 %copy.82 = bf16[4096,2048]{1,0:T(8,128)(2,1)} copy(bf16[4096,2048]{0,1:T(8,128)(2,1)} %convert_bitcast_fusion.1) | data formatting | bytes 33554432 | tf_op jit(solution)/shard_map/while | solution.py:93
  499.0 18.6 %copy.74 = bf16[16,8,64,1024]{3,2,1,0:T(8,128)(2,1)} copy(bf16[16,8,64,1024]{3,1,2,0:T(8,128)(2,1)} %all-to-all-done.1) | data formatting | bytes 33554432 | tf_op jit(solution)/shard_map/all_to_all | solution.py:80
  517.6 460.4 %while.14 = (s32[]{:T(128)}, bf16[2,64,64,1024]{3,2,1,0:T(8,128)(2,1)}, f32[2,64,8,64]{3,2,1,0:T(8,128)S(1)}, f32[2,64,8,64]{3,2,1,0:T(8,128)S(1)}, s32[2,64]{1,...) while((s32[]{:T(128)}, ...), condition=%wide.region_6.7_spmd, body=%wide.region_3.6_spmd.sunk | while | flops 2201945600 | bytes 454563776 | solution.py:93
  538.2 17.9 %gather_fusion = bf16[64,128,2048]{2,1,0:T(8,128)(2,1)} fusion(bf16[32,128,2048]{2,1,0:T(8,128)(2,1)} %get-tuple-element.192, s32[1024]{0:T(1024)S(1)} %pad_clamp_fusion.4), kind=kCustom, calls=%fused_computation.clone.1 | custom fusion | bytes 67109120 | tf_op jit(solution)/shard_map/while/body/eval_jaxpr/jit(_take)/gather | solution.py:90
  556.1 22.8 %broadcast_select_fusion.3 = bf16[64,128,2048]{2,1,0:T(8,128)(2,1)} fusion(bf16[64,128,2048]{2,1,0:T(8,128)(2,1)} %gather_fusion, pred[64]{0:T(512)(128)(4,1)S(1)} %compare_and_fusion.4), kind=kLoop, calls=%fused_computation.4.clone.1 | loop fusion | flops 16777216 | bytes 67108928 | tf_op jit(solution)/shard_map/while/body/eval_jaxpr/jit(_take)/select_n | solution.py:90
  578.9 23.7 %fusion.40 = (bf16[64,128,1024]{2,1,0:T(8,128)(2,1)}, bf16[64,128,1024]{2,1,0:T(8,128)(2,1)}) fusion(bf16[64,128,2048]{2,1,0:T(8,128)(2,1)} %broadcast_select_fusion.3), kind=kLoop, calls=%fused_computation.60.clone.1 | loop fusion | bytes 67108864 | tf_op jit(solution)/shard_map/while/body/eval_jaxpr/slice | solution.py:91
  602.6 22.4 %copy.96 = bf16[64,128,1024]{1,2,0:T(8,128)(2,1)} copy(bf16[64,128,1024]{2,1,0:T(8,128)(2,1)} %get-tuple-element.166) | data formatting | bytes 33554432 | tf_op jit(solution)/shard_map/while/body/eval_jaxpr/slice | solution.py:91
  625.0 8.4 constant_dynamic-slice_fusion.3
  633.4 8.8 copy.97
  642.3 14.3 %multiply_reduce_fusion.4 = (f32[64,8,64]{2,1,0:T(8,128)S(1)}, f32[64,8,64,128]{3,2,1,0:T(8,128)}) fusion(bf16[64,128,8,128]{1,3,2,0:T(8,128)(2,1)} %bitcast.90, bf16[64,64,8,128]{3,2,1,0:T(8,128)(2,1)} %bitcast.92), kind=kOutput, calls=%fused_computation.6.clone.1 | convolution fusion | flops 1082097664 | bytes 42074112 | tf_op jit(solution)/shard_map/while/body/eval_jaxpr/bqhd,bkhd->bhqk/dot_general | solution.py:18
  656.6 11.0 fusion.41
  667.7 22.4 %copy.95 = bf16[64,128,1024]{1,2,0:T(8,128)(2,1)} copy(bf16[64,128,1024]{2,1,0:T(8,128)(2,1)} %get-tuple-element.165) | data formatting | bytes 33554432 | tf_op jit(solution)/shard_map/while/body/eval_jaxpr/slice | solution.py:91
  690.1 19.0 %convert_bitcast_fusion.3 = bf16[64,64,8,128]{3,1,2,0:T(8,128)(2,1)} fusion(bf16[64,128,8,128]{1,3,2,0:T(8,128)(2,1)} %bitcast.89, f32[64,8,64,128]{3,2,1,0:T(8,128)} %get-tuple-element.167, f32[64,8,64]{2,1,0:T(8,128)S(1)} %get-tuple-element.168), kind=kOutput, calls=%fused_computation.12.clone.1 | convolution fusion | flops 1090519040 | bytes 42074112 | tf_op jit(solution)/shard_map/while/body/eval_jaxpr/bhqk,bkhd->bqhd/dot_general | solution.py:24
  709.1 23.4 %copy.98 = bf16[64,64,8,128]{3,2,1,0:T(8,128)(2,1)} copy(bf16[64,64,8,128]{3,1,2,0:T(8,128)(2,1)} %convert_bitcast_fusion.3) | data formatting | bytes 16777216 | tf_op jit(solution)/shard_map/while/body/eval_jaxpr/convert_element_type | solution.py:31
  732.5 13.3 convert_element_type.72
  745.8 8.4 constant_dynamic-update-slice_fusion.2
  754.2 17.9 %gather_fusion = bf16[64,128,2048]{2,1,0:T(8,128)(2,1)} fusion(bf16[32,128,2048]{2,1,0:T(8,128)(2,1)} %get-tuple-element.192, s32[1024]{0:T(1024)S(1)} %pad_clamp_fusion.4), kind=kCustom, calls=%fused_computation.clone.1 | custom fusion | bytes 67109120 | tf_op jit(solution)/shard_map/while/body/eval_jaxpr/jit(_take)/gather | solution.py:90
  772.1 22.8 %broadcast_select_fusion.3 = bf16[64,128,2048]{2,1,0:T(8,128)(2,1)} fusion(bf16[64,128,2048]{2,1,0:T(8,128)(2,1)} %gather_fusion, pred[64]{0:T(512)(128)(4,1)S(1)} %compare_and_fusion.4), kind=kLoop, calls=%fused_computation.4.clone.1 | loop fusion | flops 16777216 | bytes 67108928 | tf_op jit(solution)/shard_map/while/body/eval_jaxpr/jit(_take)/select_n | solution.py:90
  794.9 23.7 %fusion.40 = (bf16[64,128,1024]{2,1,0:T(8,128)(2,1)}, bf16[64,128,1024]{2,1,0:T(8,128)(2,1)}) fusion(bf16[64,128,2048]{2,1,0:T(8,128)(2,1)} %broadcast_select_fusion.3), kind=kLoop, calls=%fused_computation.60.clone.1 | loop fusion | bytes 67108864 | tf_op jit(solution)/shard_map/while/body/eval_jaxpr/slice | solution.py:91
  818.6 22.4 %copy.96 = bf16[64,128,1024]{1,2,0:T(8,128)(2,1)} copy(bf16[64,128,1024]{2,1,0:T(8,128)(2,1)} %get-tuple-element.166) | data formatting | bytes 33554432 | tf_op jit(solution)/shard_map/while/body/eval_jaxpr/slice | solution.py:91
  841.0 8.4 constant_dynamic-slice_fusion.3
  849.4 8.8 copy.97
  858.3 14.3 %multiply_reduce_fusion.4 = (f32[64,8,64]{2,1,0:T(8,128)S(1)}, f32[64,8,64,128]{3,2,1,0:T(8,128)}) fusion(bf16[64,128,8,128]{1,3,2,0:T(8,128)(2,1)} %bitcast.90, bf16[64,64,8,128]{3,2,1,0:T(8,128)(2,1)} %bitcast.92), kind=kOutput, calls=%fused_computation.6.clone.1 | convolution fusion | flops 1082097664 | bytes 42074112 | tf_op jit(solution)/shard_map/while/body/eval_jaxpr/bqhd,bkhd->bhqk/dot_general | solution.py:18
  872.6 11.0 fusion.41
  883.7 22.4 %copy.95 = bf16[64,128,1024]{1,2,0:T(8,128)(2,1)} copy(bf16[64,128,1024]{2,1,0:T(8,128)(2,1)} %get-tuple-element.165) | data formatting | bytes 33554432 | tf_op jit(solution)/shard_map/while/body/eval_jaxpr/slice | solution.py:91
  906.1 19.0 %convert_bitcast_fusion.3 = bf16[64,64,8,128]{3,1,2,0:T(8,128)(2,1)} fusion(bf16[64,128,8,128]{1,3,2,0:T(8,128)(2,1)} %bitcast.89, f32[64,8,64,128]{3,2,1,0:T(8,128)} %get-tuple-element.167, f32[64,8,64]{2,1,0:T(8,128)S(1)} %get-tuple-element.168), kind=kOutput, calls=%fused_computation.12.clone.1 | convolution fusion | flops 1090519040 | bytes 42074112 | tf_op jit(solution)/shard_map/while/body/eval_jaxpr/bhqk,bkhd->bqhd/dot_general | solution.py:24
  925.1 23.4 %copy.98 = bf16[64,64,8,128]{3,2,1,0:T(8,128)(2,1)} copy(bf16[64,64,8,128]{3,1,2,0:T(8,128)(2,1)} %convert_bitcast_fusion.3) | data formatting | bytes 16777216 | tf_op jit(solution)/shard_map/while/body/eval_jaxpr/convert_element_type | solution.py:31
  948.5 13.3 convert_element_type.72
  961.8 8.5 constant_dynamic-update-slice_fusion.2
  979.0 6.4 all-to-all-start.2
  985.7 7.6 all-to-all-done.2
  993.3 12.7 all_to_all.29
  1006.0 7.1 all-to-all-start.3
  1019.6 355.7 %all-to-all-done.3 = bf16[16,8,64,1024]{3,2,1,0:T(8,128)(2,1)} async-done(((bf16[16,8,64,1024]{3,2,1,0:T(8,128)(2,1)}), bf16[16,8,64,1024]{3,2,1,0:T(8,128)(2,1)}, u32[]{:S(2)}, u32[]{:S(2)}) %all-to-all-start.3) | async-done | bytes 16777248 | tf_op jit(solution)/shard_map/all_to_all | solution.py:97
  1375.3 11.3 gather_fusion.1
  1386.6 8.8 copy.84
  1395.3 8.8 multiply_reduce_fusion.1
  1404.1 4.3 divide_convert_fusion
  1408.4 7.3 convert_element_type.53
  1417.6 3.2 concatenate.11
  (72 shorter events, 23.3 us)
Async XLA Ops:
  7.6 8.8 copy-start.3
  8.2 33.2 %copy-start.5 = (s32[64]{0:T(128)}, s32[64]{0:T(128)S(1)}, u32[]{:S(2)}) copy-start(s32[64]{0:T(128)S(1)} %get-tuple-element.107) | copy-start | bytes 772
  9.8 31.5 %all-to-all-start = ((s32[16,1,8]{2,1,0:T(1,128)}), s32[16,1,8]{2,1,0:T(1,128)S(1)}, u32[]{:S(2)}, u32[]{:S(2)}) async-start(s32[16,1,8]{2,1,0:T(1,128)} %bitcast.8), calls=%async_computation | async-start | bytes 16384 | tf_op jit(solution)/shard_map/all_to_all | solution.py:81
  41.4 457.6 %all-to-all-start.1 = ((bf16[16,8,64,1024]{3,1,2,0:T(8,128)(2,1)}), bf16[16,8,64,1024]{3,1,2,0:T(8,128)(2,1)}, u32[]{:S(2)}, u32[]{:S(2)}) async-start(bf16[16,8,64,1024]{3,1,2,0:T(8,128)(2,1)} %bitcast.95), calls=%async_computation.1 | async-start | bytes 33554432 | tf_op jit(solution)/shard_map/all_to_all | solution.py:80
  47.4 179.2 %all-gather.4.cloned.1.call-start = ((), (), s32[]{:S(2)}) async-start(), calls=%async_computation.5 | async-start | bytes 1949696 | tf_op jit(solution)/shard_map/all_gather | solution.py:46
  48.1 309.8 %all-gather.6.cloned.1.call-start = ((), (), s32[]{:S(2)}) async-start(), calls=%async_computation.6 | async-start | bytes 1949696 | tf_op jit(solution)/shard_map/all_gather | solution.py:47
  48.9 403.6 %all-gather.8.cloned.1.call-start = ((), (), s32[]{:S(2)}) async-start(), calls=%async_computation.7 | async-start | bytes 11010048 | tf_op jit(solution)/shard_map/all_gather | solution.py:50
  979.0 14.3 %all-to-all-start.2 = ((f32[16,1,4096]{2,1,0:T(1,128)}), f32[16,1,4096]{2,1,0:T(1,128)S(1)}, u32[]{:S(2)}, u32[]{:S(2)}) async-start(f32[16,1,4096]{2,1,0:T(1,128)} %reshape.244), calls=%async_computation.2 | async-start | bytes 524288 | tf_op jit(solution)/shard_map/all_to_all | solution.py:99
  1006.0 7.1 copy-start
  1006.0 7.3 copy-start.2
  1006.0 7.4 copy-start.6
  1006.0 7.5 copy-start.4
  1006.0 12.3 copy-start.1
  1006.0 369.2 %all-to-all-start.3 = ((bf16[16,8,64,1024]{3,2,1,0:T(8,128)(2,1)}), bf16[16,8,64,1024]{3,2,1,0:T(8,128)(2,1)}, u32[]{:S(2)}, u32[]{:S(2)}) async-start(bf16[16,8,64,1024]{3,2,1,0:T(8,128)(2,1)} %bitcast.98), calls=%async_computation.3 | async-start | bytes 33554432 | tf_op jit(solution)/shard_map/all_to_all | solution.py:97
Sparse Core Ops, SparseCore 0:
  50.5 176.0 all-gather.3
  228.9 128.9 all-gather.5
  359.5 92.9 all-gather.7
where the time goes:
time: 1440 us; the launch traced here: 1430 us
  waiting for transfers between devices  767 us (53%)
  local copies, waits for them, and re-layouts  390 us (27%)
  matrix products  103 us (7%)
  other arithmetic  86.6 us (6%)
  loops' own time  28.3 us (2%)
  starting transfers between devices  26.5 us (2%)
    all_to_all x1, waiting for transfers between devices, local(): lax.all_to_all(partial_value, 'db', split_axis=0, concat_axis=0, tiled=True)  356 us
    all_gather x1, waiting for transfers between devices, local(): lax.all_gather(key_weight, 'db', axis=0, tiled=True)  176 us
    slice x6, local copies, waits for them, and re-layouts, one_group(): return attend(group_query, picked[..., :columns], picked[..., columns:], DH)  137 us
    all_gather x1, waiting for transfers between devices, local(): lax.all_gather(value_weight, 'db', axis=0, tiled=True)  131 us
    all_gather x1, waiting for transfers between devices, local(): piece = lax.all_gather(encodings, 'mp', axis=0, tiled=True)  94.6 us
    convert_element_type x4, local copies, waits for them, and re-layouts, attend(): partial_value.reshape(batch_size, length, columns).astype(jnp.bfloat16)  73.4 us
    select_n x4, other arithmetic, one_group(): picked = jnp.take(key_value, group_rows, axis=0)  45.6 us
    dot_general x2, matrix products, attend(): jnp.einsum('bhqk,bkhd->bqhd', expscore.astype(jnp.bfloat16), value_heads,...  38 us
  transfers between devices with their start and end apart: 7, of which 5 were waited for; matrix products, arithmetic and copies ran while one was open for 6% of the time, Pallas kernels for 0%

commit v1 on v0

--- a/solution.py
+++ b/solution.py
@@ -7,6 +7,28 @@
 DH = 128
 SPAN = 64
 SEQ = 128
+
+
+def in_order(pieces, dim):
+    pieces = jnp.moveaxis(pieces, 0, dim)
+    shape = pieces.shape
+    return pieces.reshape(*shape[:dim], shape[dim] * shape[dim + 1], *shape[dim + 2 :])
+
+
+def gather_around(x, axis, dim):
+    size = lax.axis_size(axis)
+    pairs = [(i, (i + 1) % size) for i in range(size)]
+    back = [(b, a) for a, b in pairs]
+    lower, upper = ([], [])
+    for step in range(size - 1):
+        if step % 2 == 0:
+            lower.append(lax.ppermute(lower[-1] if lower else x, axis, pairs))
+        else:
+            upper.append(lax.ppermute(upper[-1] if upper else x, axis, back))
+    blocks = jnp.stack([*lower[::-1], x, *upper])
+    shift = lax.axis_index(axis) - len(lower)
+    blocks = blocks[(jnp.arange(size) - shift) % size]
+    return in_order(blocks, dim)
 
 
 def attend(queried, key_block, value_block, head_dim):
@@ -44,7 +66,7 @@
     slots = shards * capacity
     full_keys, full_values = (
         lax.all_gather(key_weight, "db", axis=0, tiled=True),
-        lax.all_gather(value_weight, "db", axis=0, tiled=True),
+        gather_around(value_weight, "db", 0),
     )
     both_weights = jnp.concatenate([full_keys, full_values], axis=1)
     piece = lax.all_gather(encodings, "mp", axis=0, tiled=True)

time: 1440 us -> 1460 us (1.014)
  starting transfers between devices: 26.5 us -> 52.1 us
  waiting for transfers between devices: 767 us -> 744 us
    ppermute x0 -> x15, waiting for transfers between devices: none -> 380 us  [the longest x8 380 us: gather_around(): lower.append(lax.ppermute(lower[-1] if lower else x, axis, pairs))]
    all_gather x1, waiting for transfers between devices: 176 us -> 0.01 us  [local(): lax.all_gather(key_weight, 'db', axis=0, tiled=True)]
    all_gather x1 -> x0, waiting for transfers between devices: 131 us -> none  [local(): lax.all_gather(value_weight, 'db', axis=0, tiled=True)]
    all_gather x1, waiting for transfers between devices: 94.6 us -> 0.01 us  [local(): piece = lax.all_gather(encodings, 'mp', axis=0, tiled=True)]
    ppermute x0 -> x15, starting transfers between devices: none -> 25.5 us  [the longest x8 25 us: gather_around(): lower.append(lax.ppermute(lower[-1] if lower else x, axis, pairs))]
  transfers between devices with their start and end apart: 7 -> 21, of which waited for: 5 -> 10; matrix products, arithmetic and copies ran while one was open for 6% -> 6% of each run, Pallas kernels for 0% -> 0%
where the time goes in v1:
time: 1460 us; the launch traced here: 1440 us
  waiting for transfers between devices  744 us (51%)
  local copies, waits for them, and re-layouts  402 us (28%)
  matrix products  104 us (7%)
  other arithmetic  86.4 us (6%)
  starting transfers between devices  52.1 us (4%)
  loops' own time  28.3 us (2%)
    ppermute x8, waiting for transfers between devices, gather_around(): lower.append(lax.ppermute(lower[-1] if lower else x, axis, pairs))  380 us
    all_to_all x1, waiting for transfers between devices, local(): lax.all_to_all(partial_value, 'db', split_axis=0, concat_axis=0, tiled=True)  356 us
    slice x6, local copies, waits for them, and re-layouts, one_group(): return attend(group_query, picked[..., :columns], picked[..., columns:], DH)  137 us
    convert_element_type x4, local copies, waits for them, and re-layouts, attend(): partial_value.reshape(batch_size, length, columns).astype(jnp.bfloat16)  73.5 us
    select_n x4, other arithmetic, one_group(): picked = jnp.take(key_value, group_rows, axis=0)  45.6 us
    dot_general x2, matrix products, attend(): jnp.einsum('bhqk,bkhd->bqhd', expscore.astype(jnp.bfloat16), value_heads,...  38.1 us
    gather x2, local copies, waits for them, and re-layouts, one_group(): picked = jnp.take(key_value, group_rows, axis=0)  35.8 us
  transfers between devices with their start and end apart: 21, of which 10 were waited for; matrix products, arithmetic and copies ran while one was open for 6% of the time, Pallas kernels for 0%

profile of v1, /device:TPU:11, one launch (start us, length us, event | category | flops | bytes accessed | tf_op | source)
XLA Modules:
  0.0 1443.7 jit_solution(8500112173501881233)
XLA Ops:
  9.8 6.5 all-to-all-start
  23.1 5.6 reshape.238
  28.8 12.5 convolution_convert_fusion
  41.3 6.2 all-to-all-start.1
  50.5 369.6 %collective-permute-done = bf16[56,1024]{1,0:T(8,128)(2,1)S(1)} collective-permute-done((bf16[56,1024]{1,0:T(8,128)(2,1)S(1)}, bf16[56,1024]{1,0:T(8,128)(2,1)S(1)}, u32[]{:S(2)}, u32[]{:S(2)}) %collective-permute-start) | collective-permute-done | bytes 114720 | tf_op jit(solution)/shard_map/ppermute | solution.py:25
  420.0 3.4 collective-permute-start.1
  425.2 3.4 collective-permute-start.2
  430.4 3.4 collective-permute-start.3
  467.2 24.3 %convert_bitcast_fusion.1 = bf16[4096,2048]{0,1:T(8,128)(2,1)} fusion(bf16[4096,896]{1,0:T(8,128)(2,1)} %bitcast.141, bf16[896,1024]{1,0:T(8,128)(2,1)} %bitcast.134, bf16[896,1024]{1,0:T(8,128)(2,1)} %all-gather.3.cloned.1.call-done), kind=kOutput, calls=%fused_computation.29 | convolution fusion | flops 15048114176 | bytes 27787264 | tf_op jit(solution)/shard_map/dot_general | solution.py:74
  491.5 22.6 %copy.82 = bf16[4096,2048]{1,0:T(8,128)(2,1)} copy(bf16[4096,2048]{0,1:T(8,128)(2,1)} %convert_bitcast_fusion.1) | data formatting | bytes 33554432 | tf_op jit(solution)/shard_map/while | solution.py:115
  514.1 18.6 %copy.74 = bf16[16,8,64,1024]{3,2,1,0:T(8,128)(2,1)} copy(bf16[16,8,64,1024]{3,1,2,0:T(8,128)(2,1)} %all-to-all-done.1) | data formatting | bytes 33554432 | tf_op jit(solution)/shard_map/all_to_all | solution.py:102
  532.8 460.8 %while.14 = (s32[]{:T(128)}, bf16[2,64,64,1024]{3,2,1,0:T(8,128)(2,1)}, f32[2,64,8,64]{3,2,1,0:T(8,128)S(1)}, f32[2,64,8,64]{3,2,1,0:T(8,128)S(1)}, s32[2,64]{1,...) while((s32[]{:T(128)}, ...), condition=%wide.region_6.7_spmd, body=%wide.region_3.6_spmd.sunk | while | flops 2201945600 | bytes 454563776 | solution.py:115
  553.3 17.9 %gather_fusion = bf16[64,128,2048]{2,1,0:T(8,128)(2,1)} fusion(bf16[32,128,2048]{2,1,0:T(8,128)(2,1)} %get-tuple-element.192, s32[1024]{0:T(1024)S(1)} %pad_clamp_fusion.5), kind=kCustom, calls=%fused_computation.clone.1 | custom fusion | bytes 67109120 | tf_op jit(solution)/shard_map/while/body/eval_jaxpr/jit(_take)/gather | solution.py:112
  571.3 22.8 %broadcast_select_fusion.3 = bf16[64,128,2048]{2,1,0:T(8,128)(2,1)} fusion(bf16[64,128,2048]{2,1,0:T(8,128)(2,1)} %gather_fusion, pred[64]{0:T(512)(128)(4,1)S(1)} %compare_and_fusion.4), kind=kLoop, calls=%fused_computation.5.clone.1 | loop fusion | flops 16777216 | bytes 67108928 | tf_op jit(solution)/shard_map/while/body/eval_jaxpr/jit(_take)/select_n | solution.py:112
  594.1 23.8 %fusion.42 = (bf16[64,128,1024]{2,1,0:T(8,128)(2,1)}, bf16[64,128,1024]{2,1,0:T(8,128)(2,1)}) fusion(bf16[64,128,2048]{2,1,0:T(8,128)(2,1)} %broadcast_select_fusion.3), kind=kLoop, calls=%fused_computation.84.clone.1 | loop fusion | bytes 67108864 | tf_op jit(solution)/shard_map/while/body/eval_jaxpr/slice | solution.py:113
  617.8 22.3 %copy.96 = bf16[64,128,1024]{1,2,0:T(8,128)(2,1)} copy(bf16[64,128,1024]{2,1,0:T(8,128)(2,1)} %get-tuple-element.166) | data formatting | bytes 33554432 | tf_op jit(solution)/shard_map/while/body/eval_jaxpr/slice | solution.py:113
  640.2 8.4 constant_dynamic-slice_fusion.3
  648.6 8.9 copy.97
  657.5 14.4 multiply_reduce_fusion.4
  671.8 11.0 fusion.43
  682.9 22.4 %copy.95 = bf16[64,128,1024]{1,2,0:T(8,128)(2,1)} copy(bf16[64,128,1024]{2,1,0:T(8,128)(2,1)} %get-tuple-element.165) | data formatting | bytes 33554432 | tf_op jit(solution)/shard_map/while/body/eval_jaxpr/slice | solution.py:113
  705.3 19.1 %convert_bitcast_fusion.3 = bf16[64,64,8,128]{3,1,2,0:T(8,128)(2,1)} fusion(bf16[64,128,8,128]{1,3,2,0:T(8,128)(2,1)} %bitcast.124, f32[64,8,64,128]{3,2,1,0:T(8,128)} %get-tuple-element.167, f32[64,8,64]{2,1,0:T(8,128)S(1)} %get-tuple-element.168), kind=kOutput, calls=%fused_computation.13.clone.1 | convolution fusion | flops 1090519040 | bytes 42074112 | tf_op jit(solution)/shard_map/while/body/eval_jaxpr/bhqk,bkhd->bqhd/dot_general | solution.py:46
  724.4 23.4 %copy.98 = bf16[64,64,8,128]{3,2,1,0:T(8,128)(2,1)} copy(bf16[64,64,8,128]{3,1,2,0:T(8,128)(2,1)} %convert_bitcast_fusion.3) | data formatting | bytes 16777216 | tf_op jit(solution)/shard_map/while/body/eval_jaxpr/convert_element_type | solution.py:53
  747.8 13.3 convert_element_type.72
  761.1 8.4 constant_dynamic-update-slice_fusion.2
  769.5 17.9 %gather_fusion = bf16[64,128,2048]{2,1,0:T(8,128)(2,1)} fusion(bf16[32,128,2048]{2,1,0:T(8,128)(2,1)} %get-tuple-element.192, s32[1024]{0:T(1024)S(1)} %pad_clamp_fusion.5), kind=kCustom, calls=%fused_computation.clone.1 | custom fusion | bytes 67109120 | tf_op jit(solution)/shard_map/while/body/eval_jaxpr/jit(_take)/gather | solution.py:112
  787.5 22.8 %broadcast_select_fusion.3 = bf16[64,128,2048]{2,1,0:T(8,128)(2,1)} fusion(bf16[64,128,2048]{2,1,0:T(8,128)(2,1)} %gather_fusion, pred[64]{0:T(512)(128)(4,1)S(1)} %compare_and_fusion.4), kind=kLoop, calls=%fused_computation.5.clone.1 | loop fusion | flops 16777216 | bytes 67108928 | tf_op jit(solution)/shard_map/while/body/eval_jaxpr/jit(_take)/select_n | solution.py:112
  810.3 23.8 %fusion.42 = (bf16[64,128,1024]{2,1,0:T(8,128)(2,1)}, bf16[64,128,1024]{2,1,0:T(8,128)(2,1)}) fusion(bf16[64,128,2048]{2,1,0:T(8,128)(2,1)} %broadcast_select_fusion.3), kind=kLoop, calls=%fused_computation.84.clone.1 | loop fusion | bytes 67108864 | tf_op jit(solution)/shard_map/while/body/eval_jaxpr/slice | solution.py:113
  834.0 22.3 %copy.96 = bf16[64,128,1024]{1,2,0:T(8,128)(2,1)} copy(bf16[64,128,1024]{2,1,0:T(8,128)(2,1)} %get-tuple-element.166) | data formatting | bytes 33554432 | tf_op jit(solution)/shard_map/while/body/eval_jaxpr/slice | solution.py:113
  856.4 8.4 constant_dynamic-slice_fusion.3
  864.8 8.9 copy.97
  873.7 14.4 multiply_reduce_fusion.4
  888.0 11.0 fusion.43
  899.1 22.4 %copy.95 = bf16[64,128,1024]{1,2,0:T(8,128)(2,1)} copy(bf16[64,128,1024]{2,1,0:T(8,128)(2,1)} %get-tuple-element.165) | data formatting | bytes 33554432 | tf_op jit(solution)/shard_map/while/body/eval_jaxpr/slice | solution.py:113
  921.5 19.1 %convert_bitcast_fusion.3 = bf16[64,64,8,128]{3,1,2,0:T(8,128)(2,1)} fusion(bf16[64,128,8,128]{1,3,2,0:T(8,128)(2,1)} %bitcast.124, f32[64,8,64,128]{3,2,1,0:T(8,128)} %get-tuple-element.167, f32[64,8,64]{2,1,0:T(8,128)S(1)} %get-tuple-element.168), kind=kOutput, calls=%fused_computation.13.clone.1 | convolution fusion | flops 1090519040 | bytes 42074112 | tf_op jit(solution)/shard_map/while/body/eval_jaxpr/bhqk,bkhd->bqhd/dot_general | solution.py:46
  940.6 23.4 %copy.98 = bf16[64,64,8,128]{3,2,1,0:T(8,128)(2,1)} copy(bf16[64,64,8,128]{3,1,2,0:T(8,128)(2,1)} %convert_bitcast_fusion.3) | data formatting | bytes 16777216 | tf_op jit(solution)/shard_map/while/body/eval_jaxpr/convert_element_type | solution.py:53
  964.0 13.3 convert_element_type.72
  977.3 8.5 constant_dynamic-update-slice_fusion.2
  994.5 6.7 all-to-all-start.2
  1001.6 7.6 all-to-all-done.2
  1009.2 12.7 all_to_all.29
  1021.9 7.1 all-to-all-start.3
  1035.4 355.7 %all-to-all-done.3 = bf16[16,8,64,1024]{3,2,1,0:T(8,128)(2,1)} async-done(((bf16[16,8,64,1024]{3,2,1,0:T(8,128)(2,1)}), bf16[16,8,64,1024]{3,2,1,0:T(8,128)(2,1)}, u32[]{:S(2)}, u32[]{:S(2)}) %all-to-all-start.3) | async-done | bytes 16777248 | tf_op jit(solution)/shard_map/all_to_all | solution.py:119
  1391.1 11.3 gather_fusion.2
  1402.4 8.8 copy.84
  1411.2 8.8 multiply_reduce_fusion.1
  1420.0 4.3 divide_convert_fusion
  1424.3 7.3 convert_element_type.53
  (136 shorter events, 62.8 us)
Async XLA Ops:
  7.6 8.7 copy-start.12
  8.1 20.7 %copy-start.14 = (s32[64]{0:T(128)}, s32[64]{0:T(128)S(1)}, u32[]{:S(2)}) copy-start(s32[64]{0:T(128)S(1)} %get-tuple-element.107) | copy-start | bytes 772
  9.8 31.5 %all-to-all-start = ((s32[16,1,8]{2,1,0:T(1,128)}), s32[16,1,8]{2,1,0:T(1,128)S(1)}, u32[]{:S(2)}, u32[]{:S(2)}) async-start(s32[16,1,8]{2,1,0:T(1,128)} %bitcast.8), calls=%async_computation | async-start | bytes 16384 | tf_op jit(solution)/shard_map/all_to_all | solution.py:103
  41.3 7.6 copy-start
  41.3 472.8 %all-to-all-start.1 = ((bf16[16,8,64,1024]{3,1,2,0:T(8,128)(2,1)}), bf16[16,8,64,1024]{3,1,2,0:T(8,128)(2,1)}, u32[]{:S(2)}, u32[]{:S(2)}) async-start(bf16[16,8,64,1024]{3,1,2,0:T(8,128)(2,1)} %bitcast.130), calls=%async_computation.1 | async-start | bytes 33554432 | tf_op jit(solution)/shard_map/all_to_all | solution.py:102
  47.4 419.8 %all-gather.3.cloned.1.call-start = ((), (), s32[]{:S(2)}) async-start(), calls=%async_computation.5 | async-start | bytes 1949696 | tf_op jit(solution)/shard_map/all_gather | solution.py:68
  48.2 419.0 %all-gather.5.cloned.1.call-start = ((), (), s32[]{:S(2)}) async-start(), calls=%async_computation.6 | async-start | bytes 11010048 | tf_op jit(solution)/shard_map/all_gather | solution.py:72
  48.9 371.1 %collective-permute-start = (bf16[56,1024]{1,0:T(8,128)(2,1)S(1)}, bf16[56,1024]{1,0:T(8,128)(2,1)S(1)}, u32[]{:S(2)}, u32[]{:S(2)}) collective-permute-start(bf16[56,1024]{1,0:T(8,128)(2,1)S(1)} %copy-done), channel_id=1, source_target_pairs={{0,2},{2,4},{4,6},{6,8},{8,10},{10,12},{12,14},{14,16},{16,18},{18... | collective-permute-start | bytes 344072 | tf_op jit(solution)/shard_map/ppermute | solution.py:25
  420.0 5.2 collective-permute-start.1
  423.4 5.2 collective-permute-start.8
  425.2 5.2 collective-permute-start.2
  428.6 5.2 collective-permute-start.9
  430.4 8.5 copy-start.1
  430.4 5.2 collective-permute-start.3
  433.7 5.2 collective-permute-start.10
  435.5 20.4 %copy-start.4 = (bf16[56,1024]{1,0:T(8,128)(2,1)}, bf16[56,1024]{1,0:T(8,128)(2,1)S(1)}, u32[]{:S(2)}) copy-start(bf16[56,1024]{1,0:T(8,128)(2,1)S(1)} %collective-permute-done.3) | copy-start | bytes 344068
  435.5 5.2 collective-permute-start.4
  438.9 0.6 copy-start.2
  438.9 5.2 collective-permute-start.11
  440.7 15.3 %copy-start.6 = (bf16[56,1024]{1,0:T(8,128)(2,1)}, bf16[56,1024]{1,0:T(8,128)(2,1)S(1)}, u32[]{:S(2)}) copy-start(bf16[56,1024]{1,0:T(8,128)(2,1)S(1)} %collective-permute-done.4) | copy-start | bytes 344068
  440.7 5.2 collective-permute-start.5
  444.1 11.9 copy-start.3
  444.1 5.1 collective-permute-start.12
  445.8 10.2 copy-start.7
  445.9 5.2 collective-permute-start.6
  449.2 6.8 copy-start.5
  449.2 6.3 collective-permute-start.13
  451.0 5.0 copy-start.8
  451.0 5.1 collective-permute-start.7
  455.5 9.7 collective-permute-start.14
  994.5 14.6 %all-to-all-start.2 = ((f32[16,1,4096]{2,1,0:T(1,128)}), f32[16,1,4096]{2,1,0:T(1,128)S(1)}, u32[]{:S(2)}, u32[]{:S(2)}) async-start(f32[16,1,4096]{2,1,0:T(1,128)} %reshape.305), calls=%async_computation.2 | async-start | bytes 524288 | tf_op jit(solution)/shard_map/all_to_all | solution.py:121
  1021.9 7.1 copy-start.9
  1021.9 7.3 copy-start.11
  1021.9 7.4 copy-start.15
  1021.9 7.4 copy-start.13
  1021.9 12.3 copy-start.10
  1021.9 369.2 %all-to-all-start.3 = ((bf16[16,8,64,1024]{3,2,1,0:T(8,128)(2,1)}), bf16[16,8,64,1024]{3,2,1,0:T(8,128)(2,1)}, u32[]{:S(2)}, u32[]{:S(2)}) async-start(bf16[16,8,64,1024]{3,2,1,0:T(8,128)(2,1)} %bitcast.133), calls=%async_computation.3 | async-start | bytes 33554432 | tf_op jit(solution)/shard_map/all_to_all | solution.py:119
Sparse Core Ops, SparseCore 0:
  50.5 176.0 all-gather.2
  228.2 151.6 all-gather.4
